TPU v7x, 32 devices: a whole 2x2x4 slice. The times are simulated.
32 devices in a mesh: mem: 16 (over z, y, x), patch: 2 (over core).
Axes of the slice: x: 2, y: 2, z: 4, core: 2. Of those that a mesh axis runs over, the one named last changes fastest.
Arguments:
- state: bfloat16 [3, 1024, 8192], P(None, 'mem', 'patch'), may hold values from -6 to 6
- obs_noise: bfloat16 [1024, 8192], P('mem', 'patch'), may hold values from -6 to 6
- obs_values: float32 [2, 4096], P('patch', 'mem'), may hold values from -6 to 6
- obs_weights: bfloat16 [2, 32, 128, 128], P('patch', 'mem'), may hold values from -1 to 1
- tapers: float32 [8, 128, 128], replicated, may hold values from 0.2 to 1
- pair_source: int32 [2, 32, 4], P('patch', 'mem'), may hold values from 0 to 31, as said below
- pair_taper: int32 [2, 32, 4], P('patch', 'mem'), may hold values from 0 to 7
Outputs:
- analysis: bfloat16 [3, 1024, 8192], P(None, 'mem', 'patch')
Inputs may be any that keep to these rules, and one draw needn't show every extreme that they name: `pair_source`: each listed source lies in the same patch within 2 blocks of its target block; positions beyond the patch's ends are moved to its first or last block.
All inputs are finite; a program needn't handle non-finite values.
Results may differ from a plain program's by a relative error of at most 0.0058.
Values may be sent and summed in bfloat16 or wider, within the bound.
A program may use at most 64 MiB of HBM per device.

v0:
```python
import functools

import jax
import jax.numpy as jnp
from jax import lax
from jax.experimental import pallas as pl
from jax.experimental.pallas import tpu as pltpu
from jax.sharding import PartitionSpec as P

RADIUS = 2
MESH = pl.DeviceIdType.MESH


def gray(q):
    return q + (q // 2) * (1 - 2 * (q % 2))


def device_of(rank, part):
    level, q = rank // 4, rank % 4
    q = q + (level % 2) * (3 - 2 * q)
    spot = gray(q)
    return level * 4 + spot + (part % 2) * (3 - 2 * spot)


def rank_of(device, part):
    level, spot = device // 4, device % 4
    spot = spot + (part % 2) * (3 - 2 * spot)
    q = gray(spot)
    return level * 4 + q + (level % 2) * (3 - 2 * q)


def kernel(
    n,
    state, noise, obs_values, obs_weights, tapers, pair_source, pair_taper,
    out,
    rin, win_at, win_w, anom, local_t, taper_in, taper_t, outbuf, weights_in, values_in, source_in, choice_in,
    in_send, in_recv, local_sem, halo_send, halo_recv, out_send, out_recv, small_send, small_recv,
    guest_in, guest_weights, guest_values, guest_send, guest_recv, guest_local, guest_small_send, guest_small_recv,
):
    me = lax.axis_index("mem")
    part = lax.axis_index("patch")
    variables, rows, _ = state.shape
    members, owned = rin.shape[1], rin.shape[2]
    blocks, size, _ = weights_in.shape
    pairs = source_in.shape[1]
    kinds = rin.shape[0]
    rank = rank_of(me, part)
    low, high = n // 2 - 1, n // 2
    is_guest = jnp.logical_or(rank == low, rank == high)
    across = low + high - rank
    across_start = jnp.where(rank == low, RADIUS + blocks, 0)

    barrier = pltpu.get_barrier_semaphore()

    def greet(k, _):
        peer = lax.rem(me + k, n)
        pl.semaphore_signal(barrier, inc=1, device_id=(peer, part), device_id_type=MESH)
        return 0

    lax.fori_loop(1, n, greet, 0)

    def source(kind, owner):
        columns = pl.ds(pl.multiple_of(owner * owned, owned), owned)
        return noise.at[:, columns] if kind == 1 else state.at[max(kind - 1, 0), :, columns]

    my_rows = pl.ds(pl.multiple_of(me * rows, rows), rows)
    locals_ = [
        pltpu.make_async_copy(source(kind, rank), rin.at[kind, my_rows], local_sem.at[kind])
        for kind in range(kinds)
    ]
    for copy in locals_:
        copy.start()
    taper_copy = pltpu.make_async_copy(tapers, taper_in, local_sem.at[kinds])
    taper_copy.start()
    pl.semaphore_wait(barrier, n - 1)

    def guest_copy(kind):
        return pltpu.make_async_copy(
            source(kind, jnp.clip(across, 0, n - 1)), guest_in.at[kind, my_rows], guest_local.at[kind]
        )

    def send_guests(kind):
        for host, other in ((low, high), (high, low)):
            host_device = device_of(host, part)

            @pl.when(host_device != me)
            def _():
                pltpu.make_async_remote_copy(
                    src_ref=source(kind, other),
                    dst_ref=guest_in.at[kind, my_rows],
                    send_sem=guest_send.at[kind],
                    recv_sem=guest_recv.at[kind],
                    device_id=(host_device, part),
                    device_id_type=MESH,
                ).start()

        @pl.when(is_guest)
        def _():
            guest_copy(kind).start()

    guest_small = [(obs_weights.at[0], guest_weights), (obs_values, guest_values)]
    lends = jnp.logical_or(me == low, me == high)

    def guest_remote(i):
        return pltpu.make_async_remote_copy(
            src_ref=guest_small[i][0],
            dst_ref=guest_small[i][1],
            send_sem=guest_small_send.at[i],
            recv_sem=guest_small_recv.at[i],
            device_id=(device_of(jnp.clip(low + high - me, 0, n - 1), part), part),
            device_id_type=MESH,
        )

    def guest_arrived(kind):
        guest_copy(kind).wait()
        block = guest_in.at[kind, pl.ds(0, (n - 1) * rows)]
        pltpu.make_async_copy(block, block, guest_recv.at[kind]).wait()

    def send_kind(kind):
        def send(k, _):
            peer = lax.rem(me + k, n)
            pltpu.make_async_remote_copy(
                src_ref=source(kind, rank_of(peer, part)),
                dst_ref=rin.at[kind, my_rows],
                send_sem=in_send.at[kind],
                recv_sem=in_recv.at[kind],
                device_id=(peer, part),
                device_id_type=MESH,
            ).start()
            return 0

        lax.fori_loop(1, n, send, 0)

    send_kind(0)
    send_guests(0)
    keeper = device_of(me, part)
    small = [
        (obs_weights.at[0], weights_in),
        (obs_values, values_in),
        (pair_source.at[0], source_in),
        (pair_taper.at[0], choice_in),
    ]

    def small_remote(i):
        return pltpu.make_async_remote_copy(
            src_ref=small[i][0],
            dst_ref=small[i][1],
            send_sem=small_send.at[i],
            recv_sem=small_recv.at[i],
            device_id=(keeper, part),
            device_id_type=MESH,
        )

    def small_local(i):
        return pltpu.make_async_copy(small[i][0], small[i][1], small_recv.at[i])

    @pl.when(keeper != me)
    def _():
        for i in range(len(small)):
            small_remote(i).start()

    @pl.when(keeper == me)
    def _():
        for i in range(len(small)):
            small_local(i).start()

    @pl.when(lends)
    def _():
        for i in range(len(guest_small)):
            guest_remote(i).start()

    send_kind(1)
    send_guests(1)

    taper_copy.wait()
    for k in range(tapers.shape[0]):
        taper_t[k] = taper_in[k].T * (1.0 / (members - 1))

    remote_rows = (n - 1) * rows

    def arrived(kind):
        locals_[kind].wait()
        block = rin.at[kind, pl.ds(0, remote_rows)]
        pltpu.make_async_copy(block, block, in_recv.at[kind]).wait()

    def centered(array):
        values = array.astype(jnp.float32)
        center = jnp.sum(values, axis=0, keepdims=True) * (1.0 / members)
        return (values - center).astype(jnp.bfloat16)

    own = pl.ds(RADIUS, blocks)
    halo = []

    def exchange(window, index):
        left = pltpu.make_async_remote_copy(
            src_ref=window.at[own],
            dst_ref=window.at[pl.ds(RADIUS + blocks, blocks)],
            send_sem=halo_send.at[index, 0],
            recv_sem=halo_recv.at[index, 0],
            device_id=(device_of(jnp.maximum(rank - 1, 0), part), part),
            device_id_type=MESH,
        )
        right = pltpu.make_async_remote_copy(
            src_ref=window.at[own],
            dst_ref=window.at[pl.ds(0, blocks)],
            send_sem=halo_send.at[index, 1],
            recv_sem=halo_recv.at[index, 1],
            device_id=(device_of(jnp.minimum(rank + 1, n - 1), part), part),
            device_id_type=MESH,
        )

        @pl.when(jnp.logical_and(rank > 0, rank != high))
        def _():
            left.start()

        @pl.when(jnp.logical_and(rank < n - 1, rank != low))
        def _():
            right.start()

        halo.append((left, right))

    def landed(index):
        left, right = halo[index]

        @pl.when(jnp.logical_and(rank > 0, rank != high))
        def _():
            left.wait_send()
            right.wait_recv()

        @pl.when(jnp.logical_and(rank < n - 1, rank != low))
        def _():
            right.wait_send()
            left.wait_recv()

    arrived(0)
    first = centered(rin[0])
    anom[0] = first
    for b in range(blocks):
        win_at[RADIUS + b] = first[:, b * size : (b + 1) * size].T
    exchange(win_at, 0)
    send_kind(2)

    @pl.when(keeper != me)
    def _():
        for i in range(len(small)):
            small_remote(i).wait()

    @pl.when(keeper == me)
    def _():
        for i in range(len(small)):
            small_local(i).wait()

    arrived(1)

    def weigh(observed, perturbed, values, weights, start):
        innovation = (
            values[...] + perturbed.astype(jnp.float32) - observed.astype(jnp.float32)
        ).astype(jnp.bfloat16)
        for b in range(blocks):
            win_w[start + b] = lax.dot_general(
                innovation[:, b * size : (b + 1) * size],
                weights[b],
                (((1,), (1,)), ((), ())),
                preferred_element_type=jnp.float32,
            ).astype(jnp.bfloat16)

    weigh(rin[0], rin[1], values_in, weights_in, RADIUS)
    exchange(win_w, 1)

    @pl.when(is_guest)
    def _():
        guest_arrived(0)
        values = centered(guest_in[0])
        for b in range(blocks):
            win_at[across_start + b] = values[:, b * size : (b + 1) * size].T
        for i in range(len(guest_small)):
            guest_remote(i).wait_recv()
        guest_arrived(1)
        weigh(guest_in[0], guest_in[1], guest_values, guest_weights, across_start)

    @pl.when(lends)
    def _():
        for i in range(len(guest_small)):
            guest_remote(i).wait_send()

    base = rank * blocks - RADIUS

    def slot(b, j):
        return jnp.clip(source_in[b, j] - base, 0, win_at.shape[0] - 1)

    chunks = 4
    chunk = members // chunks
    per = chunk // rows
    mine = pl.ds(pl.multiple_of(rank * owned, owned), owned)
    quarter = me // per
    half, odd = quarter // 2, quarter % 2

    def localize(v):
        for b in range(blocks):
            def pair(j, _, b=b):
                covariance = jnp.dot(
                    win_at[slot(b, j)],
                    anom[v, :, b * size : (b + 1) * size],
                    preferred_element_type=jnp.float32,
                )
                local_t[v, b, pl.ds(pl.multiple_of(j * size, size), size), :] = (
                    covariance * taper_t[choice_in[b, j]]
                ).astype(jnp.bfloat16)
                return 0

            lax.fori_loop(0, pairs, pair, 0)

    def answer(v):
        kind = v + 1 if v else 0

        def step(i, _):
            over, flip = i // 2, (i + i // 2) % 2
            at = 2 * (1 - over + (2 * over - 1) * half) + flip + (1 - 2 * flip) * odd
            here = pl.ds(pl.multiple_of(at * chunk, chunk), chunk)
            for b in range(blocks):
                weights = jnp.concatenate(
                    [win_w[slot(b, j), here, :] for j in range(pairs)], axis=1
                )
                increment = jnp.dot(weights, local_t[v, b], preferred_element_type=jnp.float32)
                part_of = slice(b * size, (b + 1) * size)
                outbuf[v, here, part_of] = (
                    rin[kind, here, part_of].astype(jnp.float32) + increment
                ).astype(jnp.bfloat16)

            def give(k, _):
                peer = at * per + lax.rem(k + me, per)
                theirs = pl.ds(pl.multiple_of(peer * rows, rows), rows)

                @pl.when(peer != me)
                def _():
                    pltpu.make_async_remote_copy(
                        src_ref=outbuf.at[v, theirs, :],
                        dst_ref=out.at[v, :, mine],
                        send_sem=out_send,
                        recv_sem=out_recv,
                        device_id=(peer, part),
                        device_id_type=MESH,
                    ).start()

                return 0

            lax.fori_loop(0, per, give, 0)
            return 0

        lax.fori_loop(0, chunks, step, 0)

    for v in range(variables):
        if v:
            arrived(v + 1)
            anom[v] = centered(rin[v + 1])
        else:
            landed(0)
        localize(v)
        if not v:
            for kind in range(3, kinds):
                send_kind(kind)
            landed(1)
        answer(v)

    keep = pltpu.make_async_copy(outbuf.at[:, my_rows, :], out.at[:, :, mine], local_sem.at[kinds + 1])
    keep.start()
    keep.wait()
    for kind in range(2):
        one = guest_in.at[kind, pl.ds(0, rows)]
        both = guest_in.at[kind, pl.ds(0, 2 * rows)]

        @pl.when(is_guest)
        def _():
            pltpu.make_async_copy(one, one, guest_send.at[kind]).wait()

        @pl.when(jnp.logical_not(is_guest))
        def _():
            pltpu.make_async_copy(both, both, guest_send.at[kind]).wait()

    for kind in range(kinds):
        block = rin.at[kind, pl.ds(0, remote_rows)]
        pltpu.make_async_copy(block, block, in_send.at[kind]).wait()
    block = outbuf.at[:, pl.ds(0, remote_rows), :]
    pltpu.make_async_copy(block, block, out_send).wait()
    pltpu.make_async_copy(block, block, out_recv).wait()


def settle(array):
    parts = 6
    depth, rows, cells = array.shape
    width = cells * depth // parts

    def body(given, out, held, came, went):
        def piece(i):
            per = parts // depth
            return i // per, slice(None), pl.ds((i % per) * width, width)

        reads = [pltpu.make_async_copy(given.at[piece(i)], held.at[piece(i)], came.at[i]) for i in range(parts)]
        writes = [pltpu.make_async_copy(held.at[piece(i)], out.at[piece(i)], went.at[i]) for i in range(parts)]
        for copy in reads:
            copy.start()
        for i in range(parts):
            reads[i].wait()
            writes[i].start()
        for copy in writes:
            copy.wait()

    anywhere = pl.BlockSpec(memory_space=pl.ANY)
    return pl.pallas_call(
        body,
        out_shape=jax.ShapeDtypeStruct(array.shape, array.dtype),
        in_specs=[anywhere],
        out_specs=anywhere,
        scratch_shapes=[
            pltpu.VMEM(array.shape, array.dtype),
            pltpu.SemaphoreType.DMA((parts,)),
            pltpu.SemaphoreType.DMA((parts,)),
        ],
    )(array)


def on_device(n, state, obs_noise, obs_values, obs_weights, tapers, pair_source, pair_taper):
    variables, rows, cells = state.shape
    members = rows * n
    owned = cells // n
    blocks, size = obs_weights.shape[1], obs_weights.shape[2]
    pairs = pair_source.shape[2]
    window = blocks + 2 * RADIUS
    anywhere = pl.BlockSpec(memory_space=pl.ANY)
    kinds = variables + 1
    moved = pl.pallas_call(
        functools.partial(kernel, n),
        out_shape=jax.ShapeDtypeStruct(state.shape, state.dtype),
        in_specs=[anywhere] * 7,
        out_specs=anywhere,
        scratch_shapes=[
            pltpu.VMEM((kinds, members, owned), jnp.bfloat16),
            pltpu.VMEM((window, size, members), jnp.bfloat16),
            pltpu.VMEM((window, members, size), jnp.bfloat16),
            pltpu.VMEM((variables, members, owned), jnp.bfloat16),
            pltpu.VMEM((variables, blocks, pairs * size, size), jnp.bfloat16),
            pltpu.VMEM(tapers.shape, jnp.float32),
            pltpu.VMEM(tapers.shape, jnp.float32),
            pltpu.VMEM((variables, members, owned), jnp.bfloat16),
            pltpu.VMEM((blocks, size, size), jnp.bfloat16),
            pltpu.VMEM((1, owned), jnp.float32),
            pltpu.SMEM((blocks, pairs), jnp.int32),
            pltpu.SMEM((blocks, pairs), jnp.int32),
            pltpu.SemaphoreType.DMA((kinds,)),
            pltpu.SemaphoreType.DMA((kinds,)),
            pltpu.SemaphoreType.DMA((kinds + 2,)),
            pltpu.SemaphoreType.DMA((2, 2)),
            pltpu.SemaphoreType.DMA((2, 2)),
            pltpu.SemaphoreType.DMA,
            pltpu.SemaphoreType.DMA,
            pltpu.SemaphoreType.DMA((4,)),
            pltpu.SemaphoreType.DMA((4,)),
            pltpu.VMEM((2, members, owned), jnp.bfloat16),
            pltpu.VMEM((blocks, size, size), jnp.bfloat16),
            pltpu.VMEM((1, owned), jnp.float32),
            pltpu.SemaphoreType.DMA((2,)),
            pltpu.SemaphoreType.DMA((2,)),
            pltpu.SemaphoreType.DMA((2,)),
            pltpu.SemaphoreType.DMA((2,)),
            pltpu.SemaphoreType.DMA((2,)),
        ],
        compiler_params=pltpu.CompilerParams(collective_id=0, has_side_effects=True),
    )(state, obs_noise, obs_values, obs_weights, tapers, pair_source, pair_taper)
    return settle(moved)


def solution(mesh):
    placed = (
        P(None, "mem", "patch"),
        P("mem", "patch"),
        P("patch", "mem"),
        P("patch", "mem", None, None),
        P(),
        P("patch", "mem", None),
        P("patch", "mem", None),
    )
    return jax.shard_map(
        functools.partial(on_device, mesh.shape["mem"]),
        mesh=mesh,
        in_specs=placed,
        out_specs=P(None, "mem", "patch"),
        check_vma=False,
    )
```

profile of v0, /device:TPU:0, one launch (start us, length us, event | category | flops | bytes accessed | tf_op | source)
XLA Modules:
  0.0 92.0 jit_solution(5233147647245383056)
XLA Ops:
  0.0 89.8 %shard_map.73.given = bf16[3,64,4096]{2,1,0:T(8,128)(2,1)} custom-call(bf16[3,64,4096]{2,1,0:T(8,128)(2,1)} %state.1, bf16[64,4096]{1,0:T(8,128)(2,1)} %noise.1, f32[1,256]{1,0:T(1,128)} %obs_values.1, bf16[1,2,128,128]{3,2,1,0:T(8,128)(2,1)} %obs_weights.1, f32[8,128,128]{2,1,0:T(8,128)} %tapers.1, s32[1,2,4]{2,1,0:T(2,128)} %pair_source.1, ...), custom_call_target="tpu_custom_call" | custom-call | tf_op jit(solution)/shard_map/pallas_call | solution.py:431
  89.8 2.2 %shard_map.74 = bf16[3,64,4096]{2,1,0:T(8,128)(2,1)} custom-call(bf16[3,64,4096]{2,1,0:T(8,128)(2,1)} %shard_map.73.given), custom_call_target="tpu_custom_call" | custom-call | tf_op jit(solution)/shard_map/pallas_call | solution.py:409
where the time goes:
time: 92.9 us; the launch traced here: 92 us
  Pallas kernels  92 us (99%)
    pallas_call x1, Pallas kernels, on_device(): pl.pallas_call(functools.partial(kernel, n), out_shape=jax.ShapeDtypeStru...  89.8 us
    pallas_call x1, Pallas kernels, settle(): pl.pallas_call(body, out_shape=jax.ShapeDtypeStruct(array.shape, array.dt...  2.19 us

commit v1 on v0

v1 whole, which is shorter than its diff:
```python
import functools

import jax
import jax.numpy as jnp
from jax import lax
from jax.experimental import pallas as pl
from jax.experimental.pallas import tpu as pltpu
from jax.sharding import PartitionSpec as P

RADIUS = 2
MESH = pl.DeviceIdType.MESH


def seat_of(place, part, places):
    span = places // 4
    leg, step = place // span, place % span
    level = (leg + 1) // 2 % 2
    step = step + (leg % 2) * (span - 1 - 2 * step)
    spot = leg // 2 * span + step
    spot = spot + (part % 2) * (2 * span - 1 - 2 * spot)
    return level * 2 * span + spot


def place_of(seat, part, places):
    span = places // 4
    level, spot = seat // (2 * span), seat % (2 * span)
    spot = spot + (part % 2) * (2 * span - 1 - 2 * spot)
    side, step = spot // span, spot % span
    leg = level + side * (3 - 2 * level)
    step = step + (leg % 2) * (span - 1 - 2 * step)
    return leg * span + step


def kernel(
    n,
    state, noise, obs_values, obs_weights, tapers, pair_source, pair_taper,
    out,
    own_state, own_noise, innov, values, rin, guest_in, inn, anom, win_at, win_w, loc, taper_in, taper_t, outbuf,
    weights_in, source_in, choice_in,
    local_sem, values_send, values_recv, in_send, in_recv, guest_send, guest_recv, guest_local,
    inn_send, inn_recv, small_send, small_recv, halo_send, halo_recv, loc_send, loc_recv,
    out_send, out_recv, keep_sem,
):
    me = lax.axis_index("mem")
    part = lax.axis_index("patch")
    variables, rows, cells = state.shape
    places = n // 2
    leads_each = places // 2
    width = cells // places
    owned = cells // n
    blocks, size = obs_weights.shape[1], obs_weights.shape[2]
    per = width // size
    pairs = pair_source.shape[2]
    members = n * rows
    half, seat = me // places, me % places
    place = place_of(seat, part, places)
    leads = place // leads_each == half
    low, high = leads_each - 1, leads_each
    is_guest = jnp.logical_and(leads, jnp.logical_or(place == low, place == high))
    edge = RADIUS * size

    def device_of(side, where):
        return side * places + seat_of(where, part, places)

    def lead_of(where):
        return device_of(where // leads_each, where)

    def columns(where):
        return pl.ds(pl.multiple_of(where * width, width), width)

    barrier = pltpu.get_barrier_semaphore()

    def greet(k, _):
        peer = lax.rem(me + k, n)
        pl.semaphore_signal(barrier, inc=1, device_id=(peer, part), device_id_type=MESH)
        return 0

    lax.fori_loop(1, n, greet, 0)

    my_rows = pl.ds(pl.multiple_of(me * rows, rows), rows)
    seat_rows = pl.ds(pl.multiple_of(seat * rows, rows), rows)
    mine = columns(place)

    own_copies = [
        pltpu.make_async_copy(state.at[0], own_state, local_sem.at[variables]),
        pltpu.make_async_copy(noise, own_noise, local_sem.at[variables + 1]),
    ]
    for copy in own_copies:
        copy.start()
    taper_copy = pltpu.make_async_copy(tapers, taper_in, local_sem.at[variables + 2])
    taper_copy.start()
    my_values = values.at[:, pl.ds(pl.multiple_of(me * owned, owned), owned)]
    values_copy = pltpu.make_async_copy(obs_values, my_values, local_sem.at[variables + 3])
    values_copy.start()

    raw_local = [
        pltpu.make_async_copy(state.at[v, :, mine], rin.at[v, my_rows], local_sem.at[v]) for v in range(variables)
    ]

    @pl.when(leads)
    def _():
        for copy in raw_local:
            copy.start()

    pl.semaphore_wait(barrier, n - 1)

    def send_values(k, _):
        pltpu.make_async_remote_copy(
            src_ref=obs_values,
            dst_ref=my_values,
            send_sem=values_send,
            recv_sem=values_recv,
            device_id=(lax.rem(me + k, n), part),
            device_id_type=MESH,
        ).start()
        return 0

    lax.fori_loop(1, n, send_values, 0)

    def send_raw(v, side):
        def send(k, _):
            where = side * leads_each + lax.rem(seat + k, leads_each)
            peer = lead_of(where)

            @pl.when(peer != me)
            def _():
                pltpu.make_async_remote_copy(
                    src_ref=state.at[v, :, columns(where)],
                    dst_ref=rin.at[v, my_rows],
                    send_sem=in_send.at[v],
                    recv_sem=in_recv.at[v],
                    device_id=(peer, part),
                    device_id_type=MESH,
                ).start()

            return 0

        lax.fori_loop(0, leads_each, send, 0)

    def edge_of(host):
        start = high * width if host == low else high * width - edge
        return state.at[0, :, pl.ds(start, edge)]

    def send_guests():
        for host in (low, high):
            peer = lead_of(host)

            @pl.when(peer != me)
            def _():
                pltpu.make_async_remote_copy(
                    src_ref=edge_of(host),
                    dst_ref=guest_in.at[my_rows],
                    send_sem=guest_send,
                    recv_sem=guest_recv,
                    device_id=(peer, part),
                    device_id_type=MESH,
                ).start()

            @pl.when(peer == me)
            def _():
                pltpu.make_async_copy(edge_of(host), guest_in.at[my_rows], guest_local).start()

    send_raw(0, 1 - half)
    send_guests()
    send_raw(0, half)

    slot = me % 2
    keeper = me // 2
    small = [
        (obs_weights.at[0], weights_in),
        (pair_source.at[0], source_in),
        (pair_taper.at[0], choice_in),
    ]

    def small_remote(i, side):
        return pltpu.make_async_remote_copy(
            src_ref=small[i][0],
            dst_ref=small[i][1].at[slot],
            send_sem=small_send.at[i, side],
            recv_sem=small_recv.at[i, slot],
            device_id=(device_of(side, keeper), part),
            device_id_type=MESH,
        )

    for side in range(2):
        @pl.when(device_of(side, keeper) != me)
        def _():
            for i in range(len(small)):
                small_remote(i, side).start()

        @pl.when(device_of(side, keeper) == me)
        def _():
            for i in range(len(small)):
                pltpu.make_async_copy(small[i][0], small[i][1].at[slot], small_recv.at[i, slot]).start()

    def small_arrived():
        for i in range(len(small)):
            for s in range(2):
                here = small[i][1].at[s]
                pltpu.make_async_copy(here, here, small_recv.at[i, s]).wait()

    for copy in own_copies:
        copy.wait()
    values_copy.wait()
    others = values.at[:, pl.ds(0, (n - 1) * owned)]
    pltpu.make_async_copy(others, others, values_recv).wait()

    def innovate(p, _):
        here = columns(p)
        innov[:, here] = (
            values[:, here] + own_noise[:, here].astype(jnp.float32) - own_state[:, here].astype(jnp.float32)
        ).astype(jnp.bfloat16)
        return 0

    lax.fori_loop(0, places, innovate, 0)

    def send_innov(k, _):
        where = lax.rem(place + k, places)
        pltpu.make_async_remote_copy(
            src_ref=innov.at[:, columns(where)],
            dst_ref=inn.at[seat_rows],
            send_sem=inn_send,
            recv_sem=inn_recv,
            device_id=(device_of(half, where), part),
            device_id_type=MESH,
        ).start()
        return 0

    lax.fori_loop(1, places, send_innov, 0)
    inn_copy = pltpu.make_async_copy(innov.at[:, mine], inn.at[seat_rows], local_sem.at[variables + 4])
    inn_copy.start()
    send_raw(1, 1 - half)

    taper_copy.wait()

    def flip(k, _):
        taper_t[k] = taper_in[k].T * (1.0 / (members - 1))
        return 0

    lax.fori_loop(0, tapers.shape[0], flip, 0)

    remote_rows = pl.ds(0, (n - 1) * rows)

    def arrived(v):
        raw_local[v].wait()
        block = rin.at[v, remote_rows]
        pltpu.make_async_copy(block, block, in_recv.at[v]).wait()

    def centered(array):
        numbers = array.astype(jnp.float32)
        center = jnp.sum(numbers, axis=0, keepdims=True) * (1.0 / members)
        return (numbers - center).astype(jnp.bfloat16)

    def block_of(b):
        return pl.ds(pl.multiple_of(b * size, size), size)

    def exchange(window, index, before, after):
        left = pltpu.make_async_remote_copy(
            src_ref=window.at[pl.ds(RADIUS, RADIUS)],
            dst_ref=window.at[pl.ds(RADIUS + per, RADIUS)],
            send_sem=halo_send.at[index, 0],
            recv_sem=halo_recv.at[index, 0],
            device_id=(device_of(half, jnp.maximum(place - 1, 0)), part),
            device_id_type=MESH,
        )
        right = pltpu.make_async_remote_copy(
            src_ref=window.at[pl.ds(per, RADIUS)],
            dst_ref=window.at[pl.ds(0, RADIUS)],
            send_sem=halo_send.at[index, 1],
            recv_sem=halo_recv.at[index, 1],
            device_id=(device_of(half, jnp.minimum(place + 1, places - 1)), part),
            device_id_type=MESH,
        )

        def start():
            @pl.when(before)
            def _():
                left.start()

            @pl.when(after)
            def _():
                right.start()

        def landed():
            @pl.when(before)
            def _():
                left.wait_send()
                right.wait_recv()

            @pl.when(after)
            def _():
                right.wait_send()
                left.wait_recv()

        return start, landed

    at_start, at_landed = exchange(
        win_at,
        0,
        jnp.logical_and(leads, jnp.logical_and(place > 0, place != high)),
        jnp.logical_and(leads, jnp.logical_and(place < places - 1, place != low)),
    )
    w_start, w_landed = exchange(win_w, 1, place > 0, place < places - 1)

    @pl.when(leads)
    def _():
        arrived(0)

        def prepare(b, _):
            first = centered(rin[0, :, block_of(b)])
            anom[0, :, block_of(b)] = first
            win_at[RADIUS + b] = first.T
            return 0

        lax.fori_loop(0, per, prepare, 0)

    at_start()
    send_raw(1, half)
    send_raw(2, 1 - half)
    send_raw(2, half)
    for v in range(3, variables):
        send_raw(v, 1 - half)
        send_raw(v, half)

    small_arrived()
    inn_copy.wait()
    others_rows = inn.at[pl.ds(0, (places - 1) * rows)]
    pltpu.make_async_copy(others_rows, others_rows, inn_recv).wait()

    def weigh(b, _):
        win_w[RADIUS + b] = lax.dot_general(
            inn[:, block_of(b)],
            weights_in[b // blocks, b % blocks],
            (((1,), (1,)), ((), ())),
            preferred_element_type=jnp.float32,
        ).astype(jnp.bfloat16)
        return 0

    lax.fori_loop(0, per, weigh, 0)
    w_start()

    @pl.when(is_guest)
    def _():
        pltpu.make_async_copy(guest_in.at[my_rows], guest_in.at[my_rows], guest_local).wait()
        block = guest_in.at[remote_rows]
        pltpu.make_async_copy(block, block, guest_recv).wait()
        start = jnp.where(place == low, RADIUS + per, 0)
        for b in range(RADIUS):
            win_at[start + b] = centered(guest_in[:, b * size : (b + 1) * size]).T

    base = place * per - RADIUS

    def near(b, j):
        return jnp.clip(source_in[b // blocks, b % blocks, j] - base, 0, win_at.shape[0] - 1)

    def loc_copy(v, b):
        return pltpu.make_async_remote_copy(
            src_ref=loc.at[v, b],
            dst_ref=loc.at[v, b],
            send_sem=loc_send.at[v, b],
            recv_sem=loc_recv.at[v, b],
            device_id=(device_of(1 - half, place), part),
            device_id_type=MESH,
        )

    def localize(v):
        def step(b, _):
            for j in range(pairs):
                covariance = jnp.dot(
                    win_at[near(b, j)],
                    anom[v, :, block_of(b)],
                    preferred_element_type=jnp.float32,
                )
                loc[v, b, pl.ds(j * size, size), :] = (
                    covariance * taper_t[choice_in[b // blocks, b % blocks, j]]
                ).astype(jnp.bfloat16)
            loc_copy(v, b).start()
            return 0

        lax.fori_loop(0, per, step, 0)

    def center_all(v):
        def step(b, _):
            anom[v, :, block_of(b)] = centered(rin[v, :, block_of(b)])
            return 0

        lax.fori_loop(0, per, step, 0)

    def answer(v, b):
        weights = jnp.concatenate([win_w[near(b, j)] for j in range(pairs)], axis=1)
        increment = jnp.dot(weights, loc[v, b], preferred_element_type=jnp.float32)
        outbuf[v, :, block_of(b)] = increment.astype(jnp.bfloat16)
        there = pl.ds(pl.multiple_of(place * width + b * size, size), size)

        def give(k, _):
            peer = lax.rem(seat + k, places)
            theirs = pl.ds(pl.multiple_of(peer * rows, rows), rows)
            pltpu.make_async_remote_copy(
                src_ref=outbuf.at[v, theirs, block_of(b)],
                dst_ref=out.at[v, :, there],
                send_sem=out_send,
                recv_sem=out_recv,
                device_id=(half * places + peer, part),
                device_id_type=MESH,
            ).start()
            return 0

        lax.fori_loop(1, places, give, 0)
        pltpu.make_async_copy(outbuf.at[v, seat_rows, block_of(b)], out.at[v, :, there], keep_sem).start()

    def answers(v):
        def step(b, _):
            answer(v, b)
            return 0

        lax.fori_loop(0, per, step, 0)

    at_landed()

    @pl.when(leads)
    def _():
        localize(0)
        for v in range(1, variables):
            arrived(v)
            center_all(v)
            localize(v)

    w_landed()

    @pl.when(leads)
    def _():
        for v in range(variables):
            answers(v)

    @pl.when(jnp.logical_not(leads))
    def _():
        for v in range(variables):
            def step(b, _, v=v):
                loc_copy(v, b).wait_recv()
                answer(v, b)
                return 0

            lax.fori_loop(0, per, step, 0)

    @pl.when(leads)
    def _():
        for v in range(variables):
            def sent(b, _, v=v):
                loc_copy(v, b).wait_send()
                return 0

            lax.fori_loop(0, per, sent, 0)

    for v in range(variables):
        @pl.when(leads)
        def _():
            block = rin.at[v, pl.ds(0, (places - 1) * rows)]
            pltpu.make_async_copy(block, block, in_send.at[v]).wait()

        @pl.when(jnp.logical_not(leads))
        def _():
            block = rin.at[v, pl.ds(0, places * rows)]
            pltpu.make_async_copy(block, block, in_send.at[v]).wait()

    @pl.when(is_guest)
    def _():
        block = guest_in.at[pl.ds(0, rows)]
        pltpu.make_async_copy(block, block, guest_send).wait()

    @pl.when(jnp.logical_not(is_guest))
    def _():
        block = guest_in.at[pl.ds(0, 2 * rows)]
        pltpu.make_async_copy(block, block, guest_send).wait()

    for side in range(2):
        @pl.when(device_of(side, keeper) != me)
        def _():
            for i in range(len(small)):
                small_remote(i, side).wait_send()

    pltpu.make_async_copy(others, others, values_send).wait()
    pltpu.make_async_copy(others_rows, others_rows, inn_send).wait()
    kept = outbuf.at[:, pl.ds(0, rows), :]
    pltpu.make_async_copy(kept, kept, keep_sem).wait()
    block = outbuf.at[:, pl.ds(0, (places - 1) * rows), :]
    pltpu.make_async_copy(block, block, out_send).wait()
    pltpu.make_async_copy(block, block, out_recv).wait()


def finish(state, increment):
    parts = 6
    depth, rows, cells = state.shape
    width = cells * depth // parts

    def body(given, added, out, left, right, held, came, went):
        def piece(i):
            per = parts // depth
            return i // per, slice(None), pl.ds((i % per) * width, width)

        reads = [pltpu.make_async_copy(given.at[piece(i)], left.at[piece(i)], came.at[0, i]) for i in range(parts)]
        more = [pltpu.make_async_copy(added.at[piece(i)], right.at[piece(i)], came.at[1, i]) for i in range(parts)]
        writes = [pltpu.make_async_copy(held.at[piece(i)], out.at[piece(i)], went.at[i]) for i in range(parts)]
        for i in range(parts):
            reads[i].start()
            more[i].start()
        for i in range(parts):
            reads[i].wait()
            more[i].wait()
            held[piece(i)] = (
                left[piece(i)].astype(jnp.float32) + right[piece(i)].astype(jnp.float32)
            ).astype(jnp.bfloat16)
            writes[i].start()
        for copy in writes:
            copy.wait()

    anywhere = pl.BlockSpec(memory_space=pl.ANY)
    return pl.pallas_call(
        body,
        out_shape=jax.ShapeDtypeStruct(state.shape, state.dtype),
        in_specs=[anywhere, anywhere],
        out_specs=anywhere,
        scratch_shapes=[
            pltpu.VMEM(state.shape, state.dtype),
            pltpu.VMEM(state.shape, state.dtype),
            pltpu.VMEM(state.shape, state.dtype),
            pltpu.SemaphoreType.DMA((2, parts)),
            pltpu.SemaphoreType.DMA((parts,)),
        ],
    )(state, increment)


def on_device(n, state, obs_noise, obs_values, obs_weights, tapers, pair_source, pair_taper):
    variables, rows, cells = state.shape
    members = rows * n
    places = n // 2
    width = cells // places
    blocks, size = obs_weights.shape[1], obs_weights.shape[2]
    per = width // size
    pairs = pair_source.shape[2]
    window = per + 2 * RADIUS
    anywhere = pl.BlockSpec(memory_space=pl.ANY)
    increment = pl.pallas_call(
        functools.partial(kernel, n),
        out_shape=jax.ShapeDtypeStruct(state.shape, state.dtype),
        in_specs=[anywhere] * 7,
        out_specs=anywhere,
        scratch_shapes=[
            pltpu.VMEM((rows, cells), jnp.bfloat16),
            pltpu.VMEM((rows, cells), jnp.bfloat16),
            pltpu.VMEM((rows, cells), jnp.bfloat16),
            pltpu.VMEM((1, cells), jnp.float32),
            pltpu.VMEM((variables, members, width), jnp.bfloat16),
            pltpu.VMEM((members, RADIUS * size), jnp.bfloat16),
            pltpu.VMEM((places * rows, width), jnp.bfloat16),
            pltpu.VMEM((variables, members, width), jnp.bfloat16),
            pltpu.VMEM((window, size, members), jnp.bfloat16),
            pltpu.VMEM((window, places * rows, size), jnp.bfloat16),
            pltpu.VMEM((variables, per, pairs * size, size), jnp.bfloat16),
            pltpu.VMEM(tapers.shape, jnp.float32),
            pltpu.VMEM(tapers.shape, jnp.float32),
            pltpu.VMEM((variables, places * rows, width), jnp.bfloat16),
            pltpu.VMEM((2, blocks, size, size), jnp.bfloat16),
            pltpu.SMEM((2, blocks, pairs), jnp.int32),
            pltpu.SMEM((2, blocks, pairs), jnp.int32),
            pltpu.SemaphoreType.DMA((variables + 5,)),
            pltpu.SemaphoreType.DMA,
            pltpu.SemaphoreType.DMA,
            pltpu.SemaphoreType.DMA((variables,)),
            pltpu.SemaphoreType.DMA((variables,)),
            pltpu.SemaphoreType.DMA,
            pltpu.SemaphoreType.DMA,
            pltpu.SemaphoreType.DMA,
            pltpu.SemaphoreType.DMA,
            pltpu.SemaphoreType.DMA,
            pltpu.SemaphoreType.DMA((3, 2)),
            pltpu.SemaphoreType.DMA((3, 2)),
            pltpu.SemaphoreType.DMA((2, 2)),
            pltpu.SemaphoreType.DMA((2, 2)),
            pltpu.SemaphoreType.DMA((variables, per)),
            pltpu.SemaphoreType.DMA((variables, per)),
            pltpu.SemaphoreType.DMA,
            pltpu.SemaphoreType.DMA,
            pltpu.SemaphoreType.DMA,
        ],
        compiler_params=pltpu.CompilerParams(collective_id=0, has_side_effects=True),
    )(state, obs_noise, obs_values, obs_weights, tapers, pair_source, pair_taper)
    return finish(state, increment)


def solution(mesh):
    placed = (
        P(None, "mem", "patch"),
        P("mem", "patch"),
        P("patch", "mem"),
        P("patch", "mem", None, None),
        P(),
        P("patch", "mem", None),
        P("patch", "mem", None),
    )
    return jax.shard_map(
        functools.partial(on_device, mesh.shape["mem"]),
        mesh=mesh,
        in_specs=placed,
        out_specs=P(None, "mem", "patch"),
        check_vma=False,
    )
```

time: 92.9 us -> 88.4 us (0.952)
  Pallas kernels: 92 us -> 88.3 us
    pallas_call x1, Pallas kernels: 89.8 us -> 85.5 us  [on_device(): pl.pallas_call(functools.partial(kernel, n), out_shape=jax.ShapeDtypeStru...]
where the time goes in v1:
time: 88.4 us; the launch traced here: 88.3 us
  Pallas kernels  88.3 us (100%)
    pallas_call x1, Pallas kernels, on_device(): pl.pallas_call(functools.partial(kernel, n), out_shape=jax.ShapeDtypeStru...  85.5 us
    pallas_call x1, Pallas kernels, finish(): pl.pallas_call(body, out_shape=jax.ShapeDtypeStruct(state.shape, state.dt...  2.74 us

profile of v1, /device:TPU:0, one launch (start us, length us, event | category | flops | bytes accessed | tf_op | source)
XLA Modules:
  0.0 88.3 jit_solution(12338541869093363248)
XLA Ops:
  0.0 85.5 %shard_map.73.added = bf16[3,64,4096]{2,1,0:T(8,128)(2,1)} custom-call(bf16[3,64,4096]{2,1,0:T(8,128)(2,1)} %given.1, bf16[64,4096]{1,0:T(8,128)(2,1)} %noise.1, f32[1,256]{1,0:T(1,128)} %obs_values.1, bf16[1,2,128,128]{3,2,1,0:T(8,128)(2,1)} %obs_weights.1, f32[8,128,128]{2,1,0:T(8,128)} %tapers.1, s32[1,2,4]{2,1,0:T(2,128)} %pair_source.1, ...), custom_call_target="tpu_custom_call" | custom-call | tf_op jit(solution)/shard_map/pallas_call | solution.py:542
  85.5 2.7 %shard_map.74 = bf16[3,64,4096]{2,1,0:T(8,128)(2,1)} custom-call(bf16[3,64,4096]{2,1,0:T(8,128)(2,1)} %given.1, bf16[3,64,4096]{2,1,0:T(8,128)(2,1)} %shard_map.73.added), custom_call_target="tpu_custom_call" | custom-call | tf_op jit(solution)/shard_map/pallas_call | solution.py:517

commit v2 on v1

--- a/solution.py
+++ b/solution.py
@@ -229,7 +229,16 @@
     lax.fori_loop(1, places, send_innov, 0)
     inn_copy = pltpu.make_async_copy(innov.at[:, mine], inn.at[seat_rows], local_sem.at[variables + 4])
     inn_copy.start()
-    send_raw(1, 1 - half)
+
+    def send_rest():
+        for v in range(1, variables):
+            send_raw(v, 1 - half)
+            send_raw(v, half)
+
+    @pl.when(jnp.logical_not(leads))
+    def _():
+        send_rest()
+
 
     taper_copy.wait()
 
@@ -272,14 +281,10 @@
             device_id_type=MESH,
         )
 
-        def start():
-            @pl.when(before)
+        def start(side):
+            @pl.when((before, after)[side])
             def _():
-                left.start()
-
-            @pl.when(after)
-            def _():
-                right.start()
+                (left, right)[side].start()
 
         def landed():
             @pl.when(before)
@@ -312,15 +317,11 @@
             win_at[RADIUS + b] = first.T
             return 0
 
-        lax.fori_loop(0, per, prepare, 0)
-
-    at_start()
-    send_raw(1, half)
-    send_raw(2, 1 - half)
-    send_raw(2, half)
-    for v in range(3, variables):
-        send_raw(v, 1 - half)
-        send_raw(v, half)
+        lax.fori_loop(0, RADIUS, prepare, 0)
+        at_start(0)
+        lax.fori_loop(RADIUS, per, prepare, 0)
+        at_start(1)
+        send_rest()
 
     small_arrived()
     inn_copy.wait()
@@ -337,7 +338,9 @@
         return 0
 
     lax.fori_loop(0, per, weigh, 0)
-    w_start()
+    for side in range(2):
+        w_start(side)
+
 
     @pl.when(is_guest)
     def _():
@@ -492,40 +495,31 @@
     depth, rows, cells = state.shape
     width = cells * depth // parts
 
-    def body(given, added, out, left, right, held, came, went):
+    def body(given, added, out, held, went):
         def piece(i):
             per = parts // depth
             return i // per, slice(None), pl.ds((i % per) * width, width)
 
-        reads = [pltpu.make_async_copy(given.at[piece(i)], left.at[piece(i)], came.at[0, i]) for i in range(parts)]
-        more = [pltpu.make_async_copy(added.at[piece(i)], right.at[piece(i)], came.at[1, i]) for i in range(parts)]
         writes = [pltpu.make_async_copy(held.at[piece(i)], out.at[piece(i)], went.at[i]) for i in range(parts)]
         for i in range(parts):
-            reads[i].start()
-            more[i].start()
-        for i in range(parts):
-            reads[i].wait()
-            more[i].wait()
             held[piece(i)] = (
-                left[piece(i)].astype(jnp.float32) + right[piece(i)].astype(jnp.float32)
+                given[piece(i)].astype(jnp.float32) + added[piece(i)].astype(jnp.float32)
             ).astype(jnp.bfloat16)
             writes[i].start()
         for copy in writes:
             copy.wait()
 
-    anywhere = pl.BlockSpec(memory_space=pl.ANY)
+    near = pl.BlockSpec(memory_space=pltpu.VMEM)
     return pl.pallas_call(
         body,
         out_shape=jax.ShapeDtypeStruct(state.shape, state.dtype),
-        in_specs=[anywhere, anywhere],
-        out_specs=anywhere,
+        in_specs=[near, near],
+        out_specs=pl.BlockSpec(memory_space=pltpu.HBM),
         scratch_shapes=[
             pltpu.VMEM(state.shape, state.dtype),
-            pltpu.VMEM(state.shape, state.dtype),
-            pltpu.VMEM(state.shape, state.dtype),
-            pltpu.SemaphoreType.DMA((2, parts)),
             pltpu.SemaphoreType.DMA((parts,)),
         ],
+        compiler_params=pltpu.CompilerParams(vmem_limit_bytes=8 * 1024 * 1024),
     )(state, increment)
 
 
@@ -542,7 +536,7 @@
     increment = pl.pallas_call(
         functools.partial(kernel, n),
         out_shape=jax.ShapeDtypeStruct(state.shape, state.dtype),
-        in_specs=[anywhere] * 7,
+        in_specs=[pl.BlockSpec(memory_space=pltpu.HBM)] * 7,
         out_specs=anywhere,
         scratch_shapes=[
             pltpu.VMEM((rows, cells), jnp.bfloat16),
@@ -582,8 +576,10 @@
             pltpu.SemaphoreType.DMA,
             pltpu.SemaphoreType.DMA,
         ],
-        compiler_params=pltpu.CompilerParams(collective_id=0, has_side_effects=True),
-    )(state, obs_noise, obs_values, obs_weights, tapers, pair_source, pair_taper)
+        compiler_params=pltpu.CompilerParams(
+            collective_id=0, has_side_effects=True, vmem_limit_bytes=24 * 1024 * 1024
+        ),
+    )(*[pltpu.with_memory_space_constraint(x, pltpu.HBM) for x in (state, obs_noise, obs_values, obs_weights, tapers, pair_source, pair_taper)])
     return finish(state, increment)
 
 

time: 88.4 us -> 86.4 us (0.977)
  Pallas kernels: 88.3 us -> 86.1 us
    pallas_call x1, Pallas kernels: 2.74 us -> 1.25 us  [finish(): pl.pallas_call(body, out_shape=jax.ShapeDtypeStruct(state.shape, state.dt...]
where the time goes in v2:
time: 86.4 us; the launch traced here: 86.1 us
  Pallas kernels  86.1 us (100%)
    pallas_call x1, Pallas kernels, on_device(): pl.pallas_call(functools.partial(kernel, n), out_shape=jax.ShapeDtypeStru...  84.8 us

profile of v2, /device:TPU:0, one launch (start us, length us, event | category | flops | bytes accessed | tf_op | source)
XLA Modules:
  0.0 86.1 jit_solution(11795340856310379205)
XLA Ops:
  0.0 0.0 copy-start
  0.0 84.8 %shard_map.73.added = bf16[3,64,4096]{2,1,0:T(8,128)(2,1)S(1)} custom-call(bf16[3,64,4096]{2,1,0:T(8,128)(2,1)} %given.1, bf16[64,4096]{1,0:T(8,128)(2,1)} %noise.1, f32[1,256]{1,0:T(1,128)} %obs_values.1, bf16[1,2,128,128]{3,2,1,0:T(8,128)(2,1)} %obs_weights.1, f32[8,128,128]{2,1,0:T(8,128)} %tapers.1, s32[1,2,4]{2,1,0:T(2,128)} %pair_source.1, ...), custom_call_target="tpu_custom_call" | custom-call | tf_op jit(solution)/shard_map/pallas_call | solution.py:536
  84.8 0.0 copy-done
  84.8 1.2 %shard_map.74 = bf16[3,64,4096]{2,1,0:T(8,128)(2,1)} custom-call(bf16[3,64,4096]{2,1,0:T(8,128)(2,1)S(1)} %copy-done, bf16[3,64,4096]{2,1,0:T(8,128)(2,1)S(1)} %shard_map.73.added), custom_call_target="tpu_custom_call" | custom-call | tf_op jit(solution)/shard_map/pallas_call | solution.py:513
Async XLA Ops:
  0.0 84.8 %copy-start = (bf16[3,64,4096]{2,1,0:T(8,128)(2,1)S(1)}, bf16[3,64,4096]{2,1,0:T(8,128)(2,1)}, u32[]{:S(2)}) copy-start(bf16[3,64,4096]{2,1,0:T(8,128)(2,1)} %given.1) | copy-start | bytes 4718596

commit v3 on v2

--- a/solution.py
+++ b/solution.py
@@ -35,7 +35,7 @@
     n,
     state, noise, obs_values, obs_weights, tapers, pair_source, pair_taper,
     out,
-    own_state, own_noise, innov, values, rin, guest_in, inn, anom, win_at, win_w, loc, taper_in, taper_t, outbuf,
+    own_state, own_noise, innov, values, rin, guest_in, inn, anom, at_left, at_right, win_w, loc, taper_in, taper_t, outbuf,
     weights_in, source_in, choice_in,
     local_sem, values_send, values_recv, in_send, in_recv, guest_send, guest_recv, guest_local,
     inn_send, inn_recv, small_send, small_recv, halo_send, halo_recv, loc_send, loc_recv,
@@ -119,7 +119,7 @@
 
     def send_raw(v, side):
         def send(k, _):
-            where = side * leads_each + lax.rem(seat + k, leads_each)
+            where = side * leads_each + lax.rem(seat + seat // leads_each * (leads_each // 2) + k, leads_each)
             peer = lead_of(where)
 
             @pl.when(peer != me)
@@ -215,7 +215,7 @@
     lax.fori_loop(0, places, innovate, 0)
 
     def send_innov(k, _):
-        where = lax.rem(place + k, places)
+        where = lax.rem(place + places - k, places)
         pltpu.make_async_remote_copy(
             src_ref=innov.at[:, columns(where)],
             dst_ref=inn.at[seat_rows],
@@ -263,18 +263,18 @@
     def block_of(b):
         return pl.ds(pl.multiple_of(b * size, size), size)
 
-    def exchange(window, index, before, after):
+    def exchange(index, before, after, sources, targets):
         left = pltpu.make_async_remote_copy(
-            src_ref=window.at[pl.ds(RADIUS, RADIUS)],
-            dst_ref=window.at[pl.ds(RADIUS + per, RADIUS)],
+            src_ref=sources[0],
+            dst_ref=targets[1],
             send_sem=halo_send.at[index, 0],
             recv_sem=halo_recv.at[index, 0],
             device_id=(device_of(half, jnp.maximum(place - 1, 0)), part),
             device_id_type=MESH,
         )
         right = pltpu.make_async_remote_copy(
-            src_ref=window.at[pl.ds(per, RADIUS)],
-            dst_ref=window.at[pl.ds(0, RADIUS)],
+            src_ref=sources[1],
+            dst_ref=targets[0],
             send_sem=halo_send.at[index, 1],
             recv_sem=halo_recv.at[index, 1],
             device_id=(device_of(half, jnp.minimum(place + 1, places - 1)), part),
@@ -286,26 +286,28 @@
             def _():
                 (left, right)[side].start()
 
-        def landed():
-            @pl.when(before)
+        def landed(side):
+            @pl.when((before, after)[side])
             def _():
-                left.wait_send()
-                right.wait_recv()
-
-            @pl.when(after)
-            def _():
-                right.wait_send()
-                left.wait_recv()
+                (left, right)[side].wait_send()
+                (right, left)[side].wait_recv()
 
         return start, landed
 
     at_start, at_landed = exchange(
-        win_at,
         0,
         jnp.logical_and(leads, jnp.logical_and(place > 0, place != high)),
         jnp.logical_and(leads, jnp.logical_and(place < places - 1, place != low)),
+        (at_left.at[pl.ds(RADIUS, RADIUS)], at_right.at[pl.ds(per - RADIUS, RADIUS)]),
+        (at_left.at[pl.ds(0, RADIUS)], at_right.at[pl.ds(per, RADIUS)]),
     )
-    w_start, w_landed = exchange(win_w, 1, place > 0, place < places - 1)
+    w_start, w_landed = exchange(
+        1,
+        place > 0,
+        place < places - 1,
+        (win_w.at[pl.ds(RADIUS, RADIUS)], win_w.at[pl.ds(per, RADIUS)]),
+        (win_w.at[pl.ds(0, RADIUS)], win_w.at[pl.ds(RADIUS + per, RADIUS)]),
+    )
 
     @pl.when(leads)
     def _():
@@ -314,7 +316,9 @@
         def prepare(b, _):
             first = centered(rin[0, :, block_of(b)])
             anom[0, :, block_of(b)] = first
-            win_at[RADIUS + b] = first.T
+            flipped = first.T
+            at_left[RADIUS + b] = flipped
+            at_right[b] = flipped
             return 0
 
         lax.fori_loop(0, RADIUS, prepare, 0)
@@ -347,14 +351,29 @@
         pltpu.make_async_copy(guest_in.at[my_rows], guest_in.at[my_rows], guest_local).wait()
         block = guest_in.at[remote_rows]
         pltpu.make_async_copy(block, block, guest_recv).wait()
-        start = jnp.where(place == low, RADIUS + per, 0)
         for b in range(RADIUS):
-            win_at[start + b] = centered(guest_in[:, b * size : (b + 1) * size]).T
+            flipped = centered(guest_in[:, b * size : (b + 1) * size]).T
+
+            @pl.when(place == low)
+            def _():
+                at_right[per + b] = flipped
+
+            @pl.when(place == high)
+            def _():
+                at_left[b] = flipped
 
     base = place * per - RADIUS
 
     def near(b, j):
-        return jnp.clip(source_in[b // blocks, b % blocks, j] - base, 0, win_at.shape[0] - 1)
+        return jnp.clip(source_in[b // blocks, b % blocks, j] - base, 0, win_w.shape[0] - 1)
+
+    turned = place // (places // 4) % 2
+    bound = per // 2
+
+    def source_block(side, b, j):
+        if side:
+            return at_right[jnp.clip(near(b, j) - RADIUS, 0, at_right.shape[0] - 1)]
+        return at_left[jnp.minimum(near(b, j), at_left.shape[0] - 1)]
 
     def loc_copy(v, b):
         return pltpu.make_async_remote_copy(
@@ -366,11 +385,11 @@
             device_id_type=MESH,
         )
 
-    def localize(v):
+    def localize(v, side):
         def step(b, _):
             for j in range(pairs):
                 covariance = jnp.dot(
-                    win_at[near(b, j)],
+                    source_block(side, b, j),
                     anom[v, :, block_of(b)],
                     preferred_element_type=jnp.float32,
                 )
@@ -380,7 +399,7 @@
             loc_copy(v, b).start()
             return 0
 
-        lax.fori_loop(0, per, step, 0)
+        lax.fori_loop(side * bound, side * bound + bound, step, 0)
 
     def center_all(v):
         def step(b, _):
@@ -418,17 +437,37 @@
 
         lax.fori_loop(0, per, step, 0)
 
-    at_landed()
+    early = max(variables - 1, 1)
 
     @pl.when(leads)
     def _():
-        localize(0)
-        for v in range(1, variables):
+        def stage(k, _):
+            for side in range(2):
+                @pl.when((k + turned) % 2 == side)
+                def _():
+                    at_landed(side)
+                    localize(0, side)
+
+                    @pl.when(k == 0)
+                    def _():
+                        for v in range(1, early):
+                            arrived(v)
+                            center_all(v)
+
+                    for v in range(1, early):
+                        localize(v, side)
+
+            return 0
+
+        lax.fori_loop(0, 2, stage, 0)
+        for v in range(early, variables):
             arrived(v)
             center_all(v)
-            localize(v)
-
-    w_landed()
+            for side in range(2):
+                localize(v, side)
+
+    w_landed(0)
+    w_landed(1)
 
     @pl.when(leads)
     def _():
@@ -438,9 +477,28 @@
     @pl.when(jnp.logical_not(leads))
     def _():
         for v in range(variables):
+            block = rin.at[v, pl.ds(0, places * rows)]
+            pltpu.make_async_copy(block, block, in_send.at[v]).wait()
+
+    @pl.when(jnp.logical_not(leads))
+    def _():
+        def reply(v, b):
+            loc_copy(v, b).wait_recv()
+            answer(v, b)
+
+        def stage(k, _):
+            for v in range(early):
+                def step(i, _, v=v):
+                    reply(v, (k + turned) % 2 * bound + i)
+                    return 0
+
+                lax.fori_loop(0, bound, step, 0)
+            return 0
+
+        lax.fori_loop(0, 2, stage, 0)
+        for v in range(early, variables):
             def step(b, _, v=v):
-                loc_copy(v, b).wait_recv()
-                answer(v, b)
+                reply(v, b)
                 return 0
 
             lax.fori_loop(0, per, step, 0)
@@ -460,10 +518,6 @@
             block = rin.at[v, pl.ds(0, (places - 1) * rows)]
             pltpu.make_async_copy(block, block, in_send.at[v]).wait()
 
-        @pl.when(jnp.logical_not(leads))
-        def _():
-            block = rin.at[v, pl.ds(0, places * rows)]
-            pltpu.make_async_copy(block, block, in_send.at[v]).wait()
 
     @pl.when(is_guest)
     def _():
@@ -547,7 +601,8 @@
             pltpu.VMEM((members, RADIUS * size), jnp.bfloat16),
             pltpu.VMEM((places * rows, width), jnp.bfloat16),
             pltpu.VMEM((variables, members, width), jnp.bfloat16),
-            pltpu.VMEM((window, size, members), jnp.bfloat16),
+            pltpu.VMEM((per + RADIUS, size, members), jnp.bfloat16),
+            pltpu.VMEM((per + RADIUS, size, members), jnp.bfloat16),
             pltpu.VMEM((window, places * rows, size), jnp.bfloat16),
             pltpu.VMEM((variables, per, pairs * size, size), jnp.bfloat16),
             pltpu.VMEM(tapers.shape, jnp.float32),

time: 86.4 us -> 85.6 us (level)
  no operation moved by 1% of the time
where the time goes in v3:
time: 85.6 us; the launch traced here: 85.4 us
  Pallas kernels  85.4 us (100%)
    pallas_call x1, Pallas kernels, on_device(): pl.pallas_call(functools.partial(kernel, n), out_shape=jax.ShapeDtypeStru...  84.2 us

profile of v3, /device:TPU:0, one launch (start us, length us, event | category | flops | bytes accessed | tf_op | source)
XLA Modules:
  0.0 85.4 jit_solution(10093496132891438706)
XLA Ops:
  0.0 0.0 copy-start
  0.0 84.2 %shard_map.73.added = bf16[3,64,4096]{2,1,0:T(8,128)(2,1)S(1)} custom-call(bf16[3,64,4096]{2,1,0:T(8,128)(2,1)} %given.1, bf16[64,4096]{1,0:T(8,128)(2,1)} %noise.1, f32[1,256]{1,0:T(1,128)} %obs_values.1, bf16[1,2,128,128]{3,2,1,0:T(8,128)(2,1)} %obs_weights.1, f32[8,128,128]{2,1,0:T(8,128)} %tapers.1, s32[1,2,4]{2,1,0:T(2,128)} %pair_source.1, ...), custom_call_target="tpu_custom_call" | custom-call | tf_op jit(solution)/shard_map/pallas_call | solution.py:590
  84.2 0.0 copy-done
  84.2 1.2 %shard_map.74 = bf16[3,64,4096]{2,1,0:T(8,128)(2,1)} custom-call(bf16[3,64,4096]{2,1,0:T(8,128)(2,1)S(1)} %copy-done, bf16[3,64,4096]{2,1,0:T(8,128)(2,1)S(1)} %shard_map.73.added), custom_call_target="tpu_custom_call" | custom-call | tf_op jit(solution)/shard_map/pallas_call | solution.py:567
Async XLA Ops:
  0.0 84.2 %copy-start = (bf16[3,64,4096]{2,1,0:T(8,128)(2,1)S(1)}, bf16[3,64,4096]{2,1,0:T(8,128)(2,1)}, u32[]{:S(2)}) copy-start(bf16[3,64,4096]{2,1,0:T(8,128)(2,1)} %given.1) | copy-start | bytes 4718596

commit v4 on v3

--- a/solution.py
+++ b/solution.py
@@ -161,7 +161,6 @@
                 pltpu.make_async_copy(edge_of(host), guest_in.at[my_rows], guest_local).start()
 
     send_raw(0, 1 - half)
-    send_guests()
     send_raw(0, half)
 
     slot = me % 2
@@ -181,17 +180,6 @@
             device_id=(device_of(side, keeper), part),
             device_id_type=MESH,
         )
-
-    for side in range(2):
-        @pl.when(device_of(side, keeper) != me)
-        def _():
-            for i in range(len(small)):
-                small_remote(i, side).start()
-
-        @pl.when(device_of(side, keeper) == me)
-        def _():
-            for i in range(len(small)):
-                pltpu.make_async_copy(small[i][0], small[i][1].at[slot], small_recv.at[i, slot]).start()
 
     def small_arrived():
         for i in range(len(small)):
@@ -229,6 +217,18 @@
     lax.fori_loop(1, places, send_innov, 0)
     inn_copy = pltpu.make_async_copy(innov.at[:, mine], inn.at[seat_rows], local_sem.at[variables + 4])
     inn_copy.start()
+
+    send_guests()
+    for side in range(2):
+        @pl.when(device_of(side, keeper) != me)
+        def _():
+            for i in range(len(small)):
+                small_remote(i, side).start()
+
+        @pl.when(device_of(side, keeper) == me)
+        def _():
+            for i in range(len(small)):
+                pltpu.make_async_copy(small[i][0], small[i][1].at[slot], small_recv.at[i, slot]).start()
 
     def send_rest():
         for v in range(1, variables):

time: 85.6 us -> 85.6 us (level)
  no operation moved by 1% of the time
where the time goes in v4:
time: 85.6 us; the launch traced here: 85.4 us
  Pallas kernels  85.4 us (100%)
    pallas_call x1, Pallas kernels, on_device(): pl.pallas_call(functools.partial(kernel, n), out_shape=jax.ShapeDtypeStru...  84.2 us

profile of v4, /device:TPU:0, one launch (start us, length us, event | category | flops | bytes accessed | tf_op | source)
XLA Modules:
  0.0 85.4 jit_solution(2215647379885115181)
XLA Ops:
  0.0 0.0 copy-start
  0.0 84.2 %shard_map.73.added = bf16[3,64,4096]{2,1,0:T(8,128)(2,1)S(1)} custom-call(bf16[3,64,4096]{2,1,0:T(8,128)(2,1)} %given.1, bf16[64,4096]{1,0:T(8,128)(2,1)} %noise.1, f32[1,256]{1,0:T(1,128)} %obs_values.1, bf16[1,2,128,128]{3,2,1,0:T(8,128)(2,1)} %obs_weights.1, f32[8,128,128]{2,1,0:T(8,128)} %tapers.1, s32[1,2,4]{2,1,0:T(2,128)} %pair_source.1, ...), custom_call_target="tpu_custom_call" | custom-call | tf_op jit(solution)/shard_map/pallas_call | solution.py:590
  84.2 0.0 copy-done
  84.2 1.2 %shard_map.74 = bf16[3,64,4096]{2,1,0:T(8,128)(2,1)} custom-call(bf16[3,64,4096]{2,1,0:T(8,128)(2,1)S(1)} %copy-done, bf16[3,64,4096]{2,1,0:T(8,128)(2,1)S(1)} %shard_map.73.added), custom_call_target="tpu_custom_call" | custom-call | tf_op jit(solution)/shard_map/pallas_call | solution.py:567
Async XLA Ops:
  0.0 84.2 %copy-start = (bf16[3,64,4096]{2,1,0:T(8,128)(2,1)S(1)}, bf16[3,64,4096]{2,1,0:T(8,128)(2,1)}, u32[]{:S(2)}) copy-start(bf16[3,64,4096]{2,1,0:T(8,128)(2,1)} %given.1) | copy-start | bytes 4718596

commit v5 on v4

--- a/solution.py
+++ b/solution.py
@@ -203,7 +203,7 @@
     lax.fori_loop(0, places, innovate, 0)
 
     def send_innov(k, _):
-        where = lax.rem(place + places - k, places)
+        where = lax.rem(place + lax.rem(k + places // 2 - 2, places - 1) + 1, places)
         pltpu.make_async_remote_copy(
             src_ref=innov.at[:, columns(where)],
             dst_ref=inn.at[seat_rows],

time: 85.6 us -> 85.7 us (level)
  no operation moved by 1% of the time
where the time goes in v5:
time: 85.7 us; the launch traced here: 85.5 us
  Pallas kernels  85.5 us (100%)
    pallas_call x1, Pallas kernels, on_device(): pl.pallas_call(functools.partial(kernel, n), out_shape=jax.ShapeDtypeStru...  84.2 us

profile of v5, /device:TPU:0, one launch (start us, length us, event | category | flops | bytes accessed | tf_op | source)
XLA Modules:
  0.0 85.5 jit_solution(6827123724538545945)
XLA Ops:
  0.0 0.0 copy-start
  0.0 84.2 %shard_map.73.added = bf16[3,64,4096]{2,1,0:T(8,128)(2,1)S(1)} custom-call(bf16[3,64,4096]{2,1,0:T(8,128)(2,1)} %given.1, bf16[64,4096]{1,0:T(8,128)(2,1)} %noise.1, f32[1,256]{1,0:T(1,128)} %obs_values.1, bf16[1,2,128,128]{3,2,1,0:T(8,128)(2,1)} %obs_weights.1, f32[8,128,128]{2,1,0:T(8,128)} %tapers.1, s32[1,2,4]{2,1,0:T(2,128)} %pair_source.1, ...), custom_call_target="tpu_custom_call" | custom-call | tf_op jit(solution)/shard_map/pallas_call | solution.py:590
  84.3 0.0 copy-done
  84.3 1.2 %shard_map.74 = bf16[3,64,4096]{2,1,0:T(8,128)(2,1)} custom-call(bf16[3,64,4096]{2,1,0:T(8,128)(2,1)S(1)} %copy-done, bf16[3,64,4096]{2,1,0:T(8,128)(2,1)S(1)} %shard_map.73.added), custom_call_target="tpu_custom_call" | custom-call | tf_op jit(solution)/shard_map/pallas_call | solution.py:567
Async XLA Ops:
  0.0 84.3 %copy-start = (bf16[3,64,4096]{2,1,0:T(8,128)(2,1)S(1)}, bf16[3,64,4096]{2,1,0:T(8,128)(2,1)}, u32[]{:S(2)}) copy-start(bf16[3,64,4096]{2,1,0:T(8,128)(2,1)} %given.1) | copy-start | bytes 4718596
